TPU v7x, 256 devices: a whole 4x4x8 slice. The times are simulated.
256 devices in a mesh: tm: 32 (over z, x), elem: 8 (over y, core).
Axes of the slice: x: 4, y: 4, z: 8, core: 2. Of those that a mesh axis runs over, the one named last changes fastest.
Arguments:
- modal_coords: bfloat16 [16384, 512], P('tm'), may hold values from -6 to 6
- stress_modes: bfloat16 [3, 512, 16384], P(None, None, 'elem'), may hold values from -0.375 to 0.375
- step_decay: float32 [16384, 512], P('tm'), may hold values from 0 to 1, as said below
- ply_layup: int32 [128], P('elem'), may hold values from 0 to 15
- lin_table: float32 [16, 2], replicated, may hold values from -0.03 to 0.03
- quad_table: float32 [16, 3], replicated, may hold values from 0.0005 to 0.004
- base_index: float32 [16], replicated, may hold values from 0.9 to 1.1
Outputs:
- column_ks: float32 [16384], P('elem')
- adjoint_states: float32 [16384, 512], P('tm')
Inputs may be any that keep to these rules, and one draw needn't show every extreme that they name: `step_decay`: per-step factors of the modal adjoint states.
All inputs are finite; a program needn't handle non-finite values.
Results may differ from a plain program's by a relative error of at most 0.0027.
Values sent between devices are 32-bit elements; how exact they have to be, the bound alone decides.
A program may use at most 128 MiB of HBM per device.

v0:
```python
import jax
import jax.numpy as jnp
from jax import lax
from jax.sharding import PartitionSpec as P

COL_BLOCK = 128
LAYUPS = 16
sharpness = 100.0


def from_behind(block, axis, distance):
    devices = range(lax.axis_size(axis))
    route = [(i - distance, i) for i in devices if i - distance in devices]
    return lax.ppermute(block, axis, route)


def column_coefs(ply_layup, lin_table, quad_table, base_index):
    levels = jnp.arange(LAYUPS, dtype=jnp.int32)
    onehot = (ply_layup[:, None] == levels[None, :]).astype(jnp.float32)
    coef_table = jnp.concatenate([lin_table, quad_table, base_index[:, None]], axis=1)
    per_block = jnp.dot(onehot, coef_table, precision=lax.Precision.HIGHEST)
    return jnp.repeat(per_block, COL_BLOCK, axis=0).T


def failure_terms(stress, col_coefs):
    stress_one = stress[0]
    stress_two = stress[1]
    stress_shear = stress[2]
    lin_one = col_coefs[0][None, :]
    lin_two = col_coefs[1][None, :]
    quad_one = col_coefs[2][None, :]
    quad_two = col_coefs[3][None, :]
    quad_shear = col_coefs[4][None, :]
    static = col_coefs[5][None, :]
    cross_term = -0.5 * jnp.sqrt(quad_one * quad_two)
    failure_index = (
        static
        + lin_one * stress_one
        + lin_two * stress_two
        + quad_one * stress_one * stress_one
        + quad_two * stress_two * stress_two
        + quad_shear * stress_shear * stress_shear
        + 2.0 * cross_term * stress_one * stress_two
    )
    slopes = (
        lin_one + 2.0 * quad_one * stress_one + 2.0 * cross_term * stress_two,
        lin_two + 2.0 * quad_two * stress_two + 2.0 * cross_term * stress_one,
        2.0 * quad_shear * stress_shear,
    )
    return (failure_index, slopes)


def compose(farther, nearer):
    return (nearer[0] * farther[0], nearer[1] + nearer[0] * farther[1])


def chain_back(decay_rows, load_rows, time_axis):
    carry_scale, offset = lax.associative_scan(
        compose, (decay_rows, load_rows), reverse=True, axis=time_axis
    )
    head_carry = lax.index_in_dim(carry_scale, 0, time_axis, keepdims=False)
    head_offset = lax.index_in_dim(offset, 0, time_axis, keepdims=False)
    incoming = jnp.zeros_like(head_offset)
    for handoff_turn in range(lax.axis_size("tm") - 1):
        incoming = from_behind(head_offset + head_carry * incoming, "tm", -1)
    return offset + carry_scale * jnp.expand_dims(incoming, time_axis)


def body(modal_coords, stress_modes, step_decay, ply_layup, lin_table, quad_table, base_index):
    col_coefs = column_coefs(ply_layup, lin_table, quad_table, base_index)
    stress = jnp.einsum(
        "tm,kmc->ktc", modal_coords, stress_modes, preferred_element_type=jnp.float32
    )
    failure_index, slopes = failure_terms(stress, col_coefs)
    peak_value = lax.pmax(jnp.max(failure_index, axis=0), "tm")
    scaled_exp = jnp.exp(sharpness * (failure_index - peak_value[None, :]))
    mass_total = lax.psum(jnp.sum(scaled_exp, axis=0), "tm")
    column_ks = peak_value + jnp.log(mass_total) / sharpness
    weight = sharpness * scaled_exp / mass_total[None, :]
    sensitivity = jnp.stack([weight * slopes[0], weight * slopes[1], weight * slopes[2]]).astype(
        jnp.bfloat16
    )
    local_loads = lax.dot_general(
        sensitivity, stress_modes, (((0, 2), (0, 2)), ((), ())), preferred_element_type=jnp.float32
    )
    load_rows = lax.psum(local_loads, "elem")
    adjoint = chain_back(step_decay, load_rows, 0)
    return (column_ks, adjoint)


def solution(mesh):
    return jax.shard_map(
        body,
        mesh=mesh,
        in_specs=(P("tm", None), P(None, None, "elem"), P("tm", None), P("elem"), P(), P(), P()),
        out_specs=(P("elem"), P("tm", None)),
        check_vma=False,
    )
```

profile of v0, /device:TPU:128, one launch (start us, length us, event | category | flops | bytes accessed | tf_op | source)
XLA Modules:
  0.0 581.7 jit_solution(983731500119498555)
XLA Ops:
  8.4 5.5 convolution_bitcast_fusion
  13.9 4.3 fusion.46
  18.3 1.5 copy-done.2
  19.7 73.0 %pmax.7 = f32[2048]{0:T(1024)S(1)} all-reduce(f32[2048]{0:T(1024)S(1)} %get-tuple-element.4), channel_id=1, replica_groups=mesh['tm'=32,'elem'=8] {'tm'}, use_global_device_ids=true, to_apply=%region_1.0 | all-reduce | flops 2048 | bytes 16384 | tf_op jit(solution)/shard_map/pmax | solution.py:75
  92.7 2.9 exponential_reduce_fusion
  95.6 70.8 %psum.14 = f32[2048]{0:T(1024)S(1)} all-reduce(f32[2048]{0:T(1024)S(1)} %exponential_reduce_fusion), channel_id=1, replica_groups=mesh['tm'=32,'elem'=8] {'tm'}, use_global_device_ids=true, to_apply=%region_3.0 | all-reduce | flops 2048 | bytes 16384 | tf_op jit(solution)/shard_map/psum | solution.py:77
  166.5 7.8 %multiply_convert_fusion.2 = (bf16[1,512,2048]{2,1,0:T(8,128)(2,1)}, f32[1,512,2048]{2,1,0:T(8,128)S(1)}) fusion(f32[3,512,2048]{2,1,0:T(8,128)} %copy-done.2, f32[2048]{0:T(1024)S(1)} %bitcast.140, f32[2048]{0:T(1024)S(1)} %bitcast.123, f32[2048]{0:T(1024)S(1)} %bitcast.135, f32[2048]{0:T(1024)S(1)} %psum.14, f32[2048]{0:T(1024)S(1)} %pmax.7, ...), kind=kLoop, calls=%fused_computation.34 | loop fusion | flops 27262976 | bytes 18956288 | tf_op jit(solution)/shard_map/convert
  175.4 3.7 multiply_convert_fusion.1
  179.2 7.5 %fusion.21 = f32[512,512]{1,0:T(8,128)} fusion(bf16[3,512,2048]{2,1,0:T(8,128)(2,1)S(1)} %bitcast.58, bf16[1,512,2048]{2,1,0:T(8,128)(2,1)} %get-tuple-element.7, bf16[1,512,2048]{2,1,0:T(8,128)(2,1)} %get-tuple-element.6, bf16[1,512,2048]{2,1,0:T(8,128)(2,1)} %get-tuple-element.2), kind=kOutput, calls=%fused_computation.36 | convolution fusion | flops 3227516928 | bytes 13631488 | tf_op jit(solution)/shard_map/dot_general | solution.py:83
  188.9 2.9 slice.328
  191.9 63.0 %all-reduce.38.cloned.1.call-done = f32[512,512]{1,0:T(8,128)} async-done(((f32[512,512]{1,0:T(8,128)}), f32[512,512]{1,0:T(8,128)}) %all-reduce.38.cloned.1.call-update) | async-done | bytes 1048592 | tf_op jit(solution)/shard_map/psum | solution.py:86
  254.9 3.0 slice.329
  258.2 3.0 slice.333
  267.6 3.7 slice.325
  271.3 4.9 slice.326
  277.0 2.3 add_multiply_fusion
  279.6 4.6 pad.127
  285.0 2.7 pad.126
  288.4 4.5 collective-permute-start
  293.0 1.3 collective-permute-done
  294.3 7.5 %collective-permute-start.1 = (f32[512]{0:T(512)S(1)}, f32[512]{0:T(512)S(1)}, u32[]{:S(2)}, u32[]{:S(2)}) collective-permute-start(f32[512]{0:T(512)S(1)} %multiply_add_fusion.39), channel_id=1, source_target_pairs={{8,0},{16,8},{24,16},{32,24},{40,32},{48,40},{56,48},{64,56},{72,6... | collective-permute-start | bytes 6152 | tf_op jit(solution)/shard_map/ppermute | solution.py:14
  301.8 1.3 collective-permute-done.1
  303.0 7.5 %collective-permute-start.2 = (f32[512]{0:T(512)S(1)}, f32[512]{0:T(512)S(1)}, u32[]{:S(2)}, u32[]{:S(2)}) collective-permute-start(f32[512]{0:T(512)S(1)} %multiply_add_fusion.38), channel_id=1, source_target_pairs={{8,0},{16,8},{24,16},{32,24},{40,32},{48,40},{56,48},{64,56},{72,6... | collective-permute-start | bytes 6152 | tf_op jit(solution)/shard_map/ppermute | solution.py:14
  310.5 1.3 collective-permute-done.2
  311.8 7.5 %collective-permute-start.3 = (f32[512]{0:T(512)S(1)}, f32[512]{0:T(512)S(1)}, u32[]{:S(2)}, u32[]{:S(2)}) collective-permute-start(f32[512]{0:T(512)S(1)} %multiply_add_fusion.37), channel_id=1, source_target_pairs={{8,0},{16,8},{24,16},{32,24},{40,32},{48,40},{56,48},{64,56},{72,6... | collective-permute-start | bytes 6152 | tf_op jit(solution)/shard_map/ppermute | solution.py:14
  319.3 1.3 collective-permute-done.3
  320.6 7.5 %collective-permute-start.4 = (f32[512]{0:T(512)S(1)}, f32[512]{0:T(512)S(1)}, u32[]{:S(2)}, u32[]{:S(2)}) collective-permute-start(f32[512]{0:T(512)S(1)} %multiply_add_fusion.36), channel_id=1, source_target_pairs={{8,0},{16,8},{24,16},{32,24},{40,32},{48,40},{56,48},{64,56},{72,6... | collective-permute-start | bytes 6152 | tf_op jit(solution)/shard_map/ppermute | solution.py:14
  328.1 1.3 collective-permute-done.4
  329.4 7.5 %collective-permute-start.5 = (f32[512]{0:T(512)S(1)}, f32[512]{0:T(512)S(1)}, u32[]{:S(2)}, u32[]{:S(2)}) collective-permute-start(f32[512]{0:T(512)S(1)} %multiply_add_fusion.35), channel_id=1, source_target_pairs={{8,0},{16,8},{24,16},{32,24},{40,32},{48,40},{56,48},{64,56},{72,6... | collective-permute-start | bytes 6152 | tf_op jit(solution)/shard_map/ppermute | solution.py:14
  336.9 1.3 collective-permute-done.5
  338.2 7.5 %collective-permute-start.6 = (f32[512]{0:T(512)S(1)}, f32[512]{0:T(512)S(1)}, u32[]{:S(2)}, u32[]{:S(2)}) collective-permute-start(f32[512]{0:T(512)S(1)} %multiply_add_fusion.34), channel_id=1, source_target_pairs={{8,0},{16,8},{24,16},{32,24},{40,32},{48,40},{56,48},{64,56},{72,6... | collective-permute-start | bytes 6152 | tf_op jit(solution)/shard_map/ppermute | solution.py:14
  345.7 1.3 collective-permute-done.6
  347.0 7.5 %collective-permute-start.7 = (f32[512]{0:T(512)S(1)}, f32[512]{0:T(512)S(1)}, u32[]{:S(2)}, u32[]{:S(2)}) collective-permute-start(f32[512]{0:T(512)S(1)} %multiply_add_fusion.33), channel_id=1, source_target_pairs={{8,0},{16,8},{24,16},{32,24},{40,32},{48,40},{56,48},{64,56},{72,6... | collective-permute-start | bytes 6152 | tf_op jit(solution)/shard_map/ppermute | solution.py:14
  354.5 1.3 collective-permute-done.7
  355.8 7.5 %collective-permute-start.8 = (f32[512]{0:T(512)S(1)}, f32[512]{0:T(512)S(1)}, u32[]{:S(2)}, u32[]{:S(2)}) collective-permute-start(f32[512]{0:T(512)S(1)} %multiply_add_fusion.32), channel_id=1, source_target_pairs={{8,0},{16,8},{24,16},{32,24},{40,32},{48,40},{56,48},{64,56},{72,6... | collective-permute-start | bytes 6152 | tf_op jit(solution)/shard_map/ppermute | solution.py:14
  363.3 1.3 collective-permute-done.8
  364.6 7.5 %collective-permute-start.9 = (f32[512]{0:T(512)S(1)}, f32[512]{0:T(512)S(1)}, u32[]{:S(2)}, u32[]{:S(2)}) collective-permute-start(f32[512]{0:T(512)S(1)} %multiply_add_fusion.31), channel_id=1, source_target_pairs={{8,0},{16,8},{24,16},{32,24},{40,32},{48,40},{56,48},{64,56},{72,6... | collective-permute-start | bytes 6152 | tf_op jit(solution)/shard_map/ppermute | solution.py:14
  373.4 7.5 %collective-permute-start.10 = (f32[512]{0:T(512)S(1)}, f32[512]{0:T(512)S(1)}, u32[]{:S(2)}, u32[]{:S(2)}) collective-permute-start(f32[512]{0:T(512)S(1)} %multiply_add_fusion.30), channel_id=1, source_target_pairs={{8,0},{16,8},{24,16},{32,24},{40,32},{48,40},{56,48},{64,56},{72,6... | collective-permute-start | bytes 6152 | tf_op jit(solution)/shard_map/ppermute | solution.py:14
  382.2 7.5 %collective-permute-start.11 = (f32[512]{0:T(512)S(1)}, f32[512]{0:T(512)S(1)}, u32[]{:S(2)}, u32[]{:S(2)}) collective-permute-start(f32[512]{0:T(512)S(1)} %multiply_add_fusion.29), channel_id=1, source_target_pairs={{8,0},{16,8},{24,16},{32,24},{40,32},{48,40},{56,48},{64,56},{72,6... | collective-permute-start | bytes 6152 | tf_op jit(solution)/shard_map/ppermute | solution.py:14
  391.0 7.5 %collective-permute-start.12 = (f32[512]{0:T(512)S(1)}, f32[512]{0:T(512)S(1)}, u32[]{:S(2)}, u32[]{:S(2)}) collective-permute-start(f32[512]{0:T(512)S(1)} %multiply_add_fusion.28), channel_id=1, source_target_pairs={{8,0},{16,8},{24,16},{32,24},{40,32},{48,40},{56,48},{64,56},{72,6... | collective-permute-start | bytes 6152 | tf_op jit(solution)/shard_map/ppermute | solution.py:14
  399.8 7.5 %collective-permute-start.13 = (f32[512]{0:T(512)S(1)}, f32[512]{0:T(512)S(1)}, u32[]{:S(2)}, u32[]{:S(2)}) collective-permute-start(f32[512]{0:T(512)S(1)} %multiply_add_fusion.27), channel_id=1, source_target_pairs={{8,0},{16,8},{24,16},{32,24},{40,32},{48,40},{56,48},{64,56},{72,6... | collective-permute-start | bytes 6152 | tf_op jit(solution)/shard_map/ppermute | solution.py:14
  407.3 1.3 collective-permute-done.13
  408.6 7.5 %collective-permute-start.14 = (f32[512]{0:T(512)S(1)}, f32[512]{0:T(512)S(1)}, u32[]{:S(2)}, u32[]{:S(2)}) collective-permute-start(f32[512]{0:T(512)S(1)} %multiply_add_fusion.26), channel_id=1, source_target_pairs={{8,0},{16,8},{24,16},{32,24},{40,32},{48,40},{56,48},{64,56},{72,6... | collective-permute-start | bytes 6152 | tf_op jit(solution)/shard_map/ppermute | solution.py:14
  417.3 7.5 %collective-permute-start.15 = (f32[512]{0:T(512)S(1)}, f32[512]{0:T(512)S(1)}, u32[]{:S(2)}, u32[]{:S(2)}) collective-permute-start(f32[512]{0:T(512)S(1)} %multiply_add_fusion.25), channel_id=1, source_target_pairs={{8,0},{16,8},{24,16},{32,24},{40,32},{48,40},{56,48},{64,56},{72,6... | collective-permute-start | bytes 6152 | tf_op jit(solution)/shard_map/ppermute | solution.py:14
  426.1 7.5 %collective-permute-start.16 = (f32[512]{0:T(512)S(1)}, f32[512]{0:T(512)S(1)}, u32[]{:S(2)}, u32[]{:S(2)}) collective-permute-start(f32[512]{0:T(512)S(1)} %multiply_add_fusion.24), channel_id=1, source_target_pairs={{8,0},{16,8},{24,16},{32,24},{40,32},{48,40},{56,48},{64,56},{72,6... | collective-permute-start | bytes 6152 | tf_op jit(solution)/shard_map/ppermute | solution.py:14
  434.9 7.5 %collective-permute-start.17 = (f32[512]{0:T(512)S(1)}, f32[512]{0:T(512)S(1)}, u32[]{:S(2)}, u32[]{:S(2)}) collective-permute-start(f32[512]{0:T(512)S(1)} %multiply_add_fusion.23), channel_id=1, source_target_pairs={{8,0},{16,8},{24,16},{32,24},{40,32},{48,40},{56,48},{64,56},{72,6... | collective-permute-start | bytes 6152 | tf_op jit(solution)/shard_map/ppermute | solution.py:14
  443.7 7.5 %collective-permute-start.18 = (f32[512]{0:T(512)S(1)}, f32[512]{0:T(512)S(1)}, u32[]{:S(2)}, u32[]{:S(2)}) collective-permute-start(f32[512]{0:T(512)S(1)} %multiply_add_fusion.22), channel_id=1, source_target_pairs={{8,0},{16,8},{24,16},{32,24},{40,32},{48,40},{56,48},{64,56},{72,6... | collective-permute-start | bytes 6152 | tf_op jit(solution)/shard_map/ppermute | solution.py:14
  452.5 7.5 %collective-permute-start.19 = (f32[512]{0:T(512)S(1)}, f32[512]{0:T(512)S(1)}, u32[]{:S(2)}, u32[]{:S(2)}) collective-permute-start(f32[512]{0:T(512)S(1)} %multiply_add_fusion.21), channel_id=1, source_target_pairs={{8,0},{16,8},{24,16},{32,24},{40,32},{48,40},{56,48},{64,56},{72,6... | collective-permute-start | bytes 6152 | tf_op jit(solution)/shard_map/ppermute | solution.py:14
  461.3 7.5 %collective-permute-start.20 = (f32[512]{0:T(512)S(1)}, f32[512]{0:T(512)S(1)}, u32[]{:S(2)}, u32[]{:S(2)}) collective-permute-start(f32[512]{0:T(512)S(1)} %multiply_add_fusion.20), channel_id=1, source_target_pairs={{8,0},{16,8},{24,16},{32,24},{40,32},{48,40},{56,48},{64,56},{72,6... | collective-permute-start | bytes 6152 | tf_op jit(solution)/shard_map/ppermute | solution.py:14
  468.8 1.3 collective-permute-done.20
  470.1 7.5 %collective-permute-start.21 = (f32[512]{0:T(512)S(1)}, f32[512]{0:T(512)S(1)}, u32[]{:S(2)}, u32[]{:S(2)}) collective-permute-start(f32[512]{0:T(512)S(1)} %multiply_add_fusion.19), channel_id=1, source_target_pairs={{8,0},{16,8},{24,16},{32,24},{40,32},{48,40},{56,48},{64,56},{72,6... | collective-permute-start | bytes 6152 | tf_op jit(solution)/shard_map/ppermute | solution.py:14
  478.9 7.5 %collective-permute-start.22 = (f32[512]{0:T(512)S(1)}, f32[512]{0:T(512)S(1)}, u32[]{:S(2)}, u32[]{:S(2)}) collective-permute-start(f32[512]{0:T(512)S(1)} %multiply_add_fusion.18), channel_id=1, source_target_pairs={{8,0},{16,8},{24,16},{32,24},{40,32},{48,40},{56,48},{64,56},{72,6... | collective-permute-start | bytes 6152 | tf_op jit(solution)/shard_map/ppermute | solution.py:14
  487.7 7.5 %collective-permute-start.23 = (f32[512]{0:T(512)S(1)}, f32[512]{0:T(512)S(1)}, u32[]{:S(2)}, u32[]{:S(2)}) collective-permute-start(f32[512]{0:T(512)S(1)} %multiply_add_fusion.17), channel_id=1, source_target_pairs={{8,0},{16,8},{24,16},{32,24},{40,32},{48,40},{56,48},{64,56},{72,6... | collective-permute-start | bytes 6152 | tf_op jit(solution)/shard_map/ppermute | solution.py:14
  496.5 7.5 %collective-permute-start.24 = (f32[512]{0:T(512)S(1)}, f32[512]{0:T(512)S(1)}, u32[]{:S(2)}, u32[]{:S(2)}) collective-permute-start(f32[512]{0:T(512)S(1)} %multiply_add_fusion.16), channel_id=1, source_target_pairs={{8,0},{16,8},{24,16},{32,24},{40,32},{48,40},{56,48},{64,56},{72,6... | collective-permute-start | bytes 6152 | tf_op jit(solution)/shard_map/ppermute | solution.py:14
  505.3 7.5 %collective-permute-start.25 = (f32[512]{0:T(512)S(1)}, f32[512]{0:T(512)S(1)}, u32[]{:S(2)}, u32[]{:S(2)}) collective-permute-start(f32[512]{0:T(512)S(1)} %multiply_add_fusion.15), channel_id=1, source_target_pairs={{8,0},{16,8},{24,16},{32,24},{40,32},{48,40},{56,48},{64,56},{72,6... | collective-permute-start | bytes 6152 | tf_op jit(solution)/shard_map/ppermute | solution.py:14
  514.1 7.5 %collective-permute-start.26 = (f32[512]{0:T(512)S(1)}, f32[512]{0:T(512)S(1)}, u32[]{:S(2)}, u32[]{:S(2)}) collective-permute-start(f32[512]{0:T(512)S(1)} %multiply_add_fusion.14), channel_id=1, source_target_pairs={{8,0},{16,8},{24,16},{32,24},{40,32},{48,40},{56,48},{64,56},{72,6... | collective-permute-start | bytes 6152 | tf_op jit(solution)/shard_map/ppermute | solution.py:14
  522.9 7.5 %collective-permute-start.27 = (f32[512]{0:T(512)S(1)}, f32[512]{0:T(512)S(1)}, u32[]{:S(2)}, u32[]{:S(2)}) collective-permute-start(f32[512]{0:T(512)S(1)} %multiply_add_fusion.13), channel_id=1, source_target_pairs={{8,0},{16,8},{24,16},{32,24},{40,32},{48,40},{56,48},{64,56},{72,6... | collective-permute-start | bytes 6152 | tf_op jit(solution)/shard_map/ppermute | solution.py:14
  531.7 7.5 %collective-permute-start.28 = (f32[512]{0:T(512)S(1)}, f32[512]{0:T(512)S(1)}, u32[]{:S(2)}, u32[]{:S(2)}) collective-permute-start(f32[512]{0:T(512)S(1)} %multiply_add_fusion.12), channel_id=1, source_target_pairs={{8,0},{16,8},{24,16},{32,24},{40,32},{48,40},{56,48},{64,56},{72,6... | collective-permute-start | bytes 6152 | tf_op jit(solution)/shard_map/ppermute | solution.py:14
  540.4 7.5 %collective-permute-start.29 = (f32[512]{0:T(512)S(1)}, f32[512]{0:T(512)S(1)}, u32[]{:S(2)}, u32[]{:S(2)}) collective-permute-start(f32[512]{0:T(512)S(1)} %multiply_add_fusion.11), channel_id=1, source_target_pairs={{8,0},{16,8},{24,16},{32,24},{40,32},{48,40},{56,48},{64,56},{72,6... | collective-permute-start | bytes 6152 | tf_op jit(solution)/shard_map/ppermute | solution.py:14
  549.2 7.5 %collective-permute-start.30 = (f32[512]{0:T(512)S(1)}, f32[512]{0:T(512)S(1)}, u32[]{:S(2)}, u32[]{:S(2)}) collective-permute-start(f32[512]{0:T(512)S(1)} %multiply_add_fusion.10), channel_id=1, source_target_pairs={{8,0},{16,8},{24,16},{32,24},{40,32},{48,40},{56,48},{64,56},{72,6... | collective-permute-start | bytes 6152 | tf_op jit(solution)/shard_map/ppermute | solution.py:14
  558.6 1.8 add.404
  560.4 6.9 %rev.9 = f32[512,512]{1,0:T(8,128)S(1)} reverse(f32[512,512]{1,0:T(8,128)} %add.413), dimensions={0} | reverse | bytes 2097152 | tf_op jit(solution)/shard_map/rev | solution.py:58
  567.2 5.2 rev.8
  572.4 2.4 multiply_add_fusion
  (214 shorter events, 39.6 us)
Async XLA Ops:
  7.2 1.2 copy-start
  7.2 247.7 %all-reduce.38.cloned.1.call-start = ((), (), s32[]{:S(2)}) async-start(), calls=%async_computation | async-start | bytes 2097152 | tf_op jit(solution)/shard_map/psum | solution.py:86
  13.9 5.8 copy-start.2
  166.4 9.0 %copy-start.3 = (f32[3,512,2048]{2,1,0:T(8,128)S(1)}, f32[3,512,2048]{2,1,0:T(8,128)}, u32[]{:S(2)}) copy-start(f32[3,512,2048]{2,1,0:T(8,128)} %copy-done.2) | copy-start | bytes 37748740
  166.5 12.7 %slice-start = ((s8[6291456]{0:T(1024)(128)(4,1)}), s8[4194304]{0:T(1024)(128)(4,1)S(1)}, s32[]{:S(2)}) async-start(s8[6291456]{0:T(1024)(128)(4,1)} %bitcast.57), calls=%async_computation.1 | async-start | bytes 8388608
  175.4 3.7 slice-start.1
  179.1 7.5 %copy-start.4 = (f32[512,512]{1,0:T(8,128)S(1)}, f32[512,512]{1,0:T(8,128)}, u32[]{:S(2)}) copy-start(f32[512,512]{1,0:T(8,128)} %param.9) | copy-start | bytes 3145732
  279.4 5.6 copy-start.5
  288.4 5.8 collective-permute-start
  294.3 8.8 %collective-permute-start.1 = (f32[512]{0:T(512)S(1)}, f32[512]{0:T(512)S(1)}, u32[]{:S(2)}, u32[]{:S(2)}) collective-permute-start(f32[512]{0:T(512)S(1)} %multiply_add_fusion.39), channel_id=1, source_target_pairs={{8,0},{16,8},{24,16},{32,24},{40,32},{48,40},{56,48},{64,56},{72,6... | collective-permute-start | bytes 6152 | tf_op jit(solution)/shard_map/ppermute | solution.py:14
  303.0 8.8 %collective-permute-start.2 = (f32[512]{0:T(512)S(1)}, f32[512]{0:T(512)S(1)}, u32[]{:S(2)}, u32[]{:S(2)}) collective-permute-start(f32[512]{0:T(512)S(1)} %multiply_add_fusion.38), channel_id=1, source_target_pairs={{8,0},{16,8},{24,16},{32,24},{40,32},{48,40},{56,48},{64,56},{72,6... | collective-permute-start | bytes 6152 | tf_op jit(solution)/shard_map/ppermute | solution.py:14
  311.8 8.8 %collective-permute-start.3 = (f32[512]{0:T(512)S(1)}, f32[512]{0:T(512)S(1)}, u32[]{:S(2)}, u32[]{:S(2)}) collective-permute-start(f32[512]{0:T(512)S(1)} %multiply_add_fusion.37), channel_id=1, source_target_pairs={{8,0},{16,8},{24,16},{32,24},{40,32},{48,40},{56,48},{64,56},{72,6... | collective-permute-start | bytes 6152 | tf_op jit(solution)/shard_map/ppermute | solution.py:14
  320.6 8.8 %collective-permute-start.4 = (f32[512]{0:T(512)S(1)}, f32[512]{0:T(512)S(1)}, u32[]{:S(2)}, u32[]{:S(2)}) collective-permute-start(f32[512]{0:T(512)S(1)} %multiply_add_fusion.36), channel_id=1, source_target_pairs={{8,0},{16,8},{24,16},{32,24},{40,32},{48,40},{56,48},{64,56},{72,6... | collective-permute-start | bytes 6152 | tf_op jit(solution)/shard_map/ppermute | solution.py:14
  329.4 8.8 %collective-permute-start.5 = (f32[512]{0:T(512)S(1)}, f32[512]{0:T(512)S(1)}, u32[]{:S(2)}, u32[]{:S(2)}) collective-permute-start(f32[512]{0:T(512)S(1)} %multiply_add_fusion.35), channel_id=1, source_target_pairs={{8,0},{16,8},{24,16},{32,24},{40,32},{48,40},{56,48},{64,56},{72,6... | collective-permute-start | bytes 6152 | tf_op jit(solution)/shard_map/ppermute | solution.py:14
  338.2 8.8 %collective-permute-start.6 = (f32[512]{0:T(512)S(1)}, f32[512]{0:T(512)S(1)}, u32[]{:S(2)}, u32[]{:S(2)}) collective-permute-start(f32[512]{0:T(512)S(1)} %multiply_add_fusion.34), channel_id=1, source_target_pairs={{8,0},{16,8},{24,16},{32,24},{40,32},{48,40},{56,48},{64,56},{72,6... | collective-permute-start | bytes 6152 | tf_op jit(solution)/shard_map/ppermute | solution.py:14
  347.0 8.8 %collective-permute-start.7 = (f32[512]{0:T(512)S(1)}, f32[512]{0:T(512)S(1)}, u32[]{:S(2)}, u32[]{:S(2)}) collective-permute-start(f32[512]{0:T(512)S(1)} %multiply_add_fusion.33), channel_id=1, source_target_pairs={{8,0},{16,8},{24,16},{32,24},{40,32},{48,40},{56,48},{64,56},{72,6... | collective-permute-start | bytes 6152 | tf_op jit(solution)/shard_map/ppermute | solution.py:14
  355.8 8.8 %collective-permute-start.8 = (f32[512]{0:T(512)S(1)}, f32[512]{0:T(512)S(1)}, u32[]{:S(2)}, u32[]{:S(2)}) collective-permute-start(f32[512]{0:T(512)S(1)} %multiply_add_fusion.32), channel_id=1, source_target_pairs={{8,0},{16,8},{24,16},{32,24},{40,32},{48,40},{56,48},{64,56},{72,6... | collective-permute-start | bytes 6152 | tf_op jit(solution)/shard_map/ppermute | solution.py:14
  364.6 8.8 %collective-permute-start.9 = (f32[512]{0:T(512)S(1)}, f32[512]{0:T(512)S(1)}, u32[]{:S(2)}, u32[]{:S(2)}) collective-permute-start(f32[512]{0:T(512)S(1)} %multiply_add_fusion.31), channel_id=1, source_target_pairs={{8,0},{16,8},{24,16},{32,24},{40,32},{48,40},{56,48},{64,56},{72,6... | collective-permute-start | bytes 6152 | tf_op jit(solution)/shard_map/ppermute | solution.py:14
  373.4 8.8 %collective-permute-start.10 = (f32[512]{0:T(512)S(1)}, f32[512]{0:T(512)S(1)}, u32[]{:S(2)}, u32[]{:S(2)}) collective-permute-start(f32[512]{0:T(512)S(1)} %multiply_add_fusion.30), channel_id=1, source_target_pairs={{8,0},{16,8},{24,16},{32,24},{40,32},{48,40},{56,48},{64,56},{72,6... | collective-permute-start | bytes 6152 | tf_op jit(solution)/shard_map/ppermute | solution.py:14
  382.2 8.8 %collective-permute-start.11 = (f32[512]{0:T(512)S(1)}, f32[512]{0:T(512)S(1)}, u32[]{:S(2)}, u32[]{:S(2)}) collective-permute-start(f32[512]{0:T(512)S(1)} %multiply_add_fusion.29), channel_id=1, source_target_pairs={{8,0},{16,8},{24,16},{32,24},{40,32},{48,40},{56,48},{64,56},{72,6... | collective-permute-start | bytes 6152 | tf_op jit(solution)/shard_map/ppermute | solution.py:14
  391.0 8.8 %collective-permute-start.12 = (f32[512]{0:T(512)S(1)}, f32[512]{0:T(512)S(1)}, u32[]{:S(2)}, u32[]{:S(2)}) collective-permute-start(f32[512]{0:T(512)S(1)} %multiply_add_fusion.28), channel_id=1, source_target_pairs={{8,0},{16,8},{24,16},{32,24},{40,32},{48,40},{56,48},{64,56},{72,6... | collective-permute-start | bytes 6152 | tf_op jit(solution)/shard_map/ppermute | solution.py:14
  399.8 8.8 %collective-permute-start.13 = (f32[512]{0:T(512)S(1)}, f32[512]{0:T(512)S(1)}, u32[]{:S(2)}, u32[]{:S(2)}) collective-permute-start(f32[512]{0:T(512)S(1)} %multiply_add_fusion.27), channel_id=1, source_target_pairs={{8,0},{16,8},{24,16},{32,24},{40,32},{48,40},{56,48},{64,56},{72,6... | collective-permute-start | bytes 6152 | tf_op jit(solution)/shard_map/ppermute | solution.py:14
  408.6 8.8 %collective-permute-start.14 = (f32[512]{0:T(512)S(1)}, f32[512]{0:T(512)S(1)}, u32[]{:S(2)}, u32[]{:S(2)}) collective-permute-start(f32[512]{0:T(512)S(1)} %multiply_add_fusion.26), channel_id=1, source_target_pairs={{8,0},{16,8},{24,16},{32,24},{40,32},{48,40},{56,48},{64,56},{72,6... | collective-permute-start | bytes 6152 | tf_op jit(solution)/shard_map/ppermute | solution.py:14
  417.3 8.8 %collective-permute-start.15 = (f32[512]{0:T(512)S(1)}, f32[512]{0:T(512)S(1)}, u32[]{:S(2)}, u32[]{:S(2)}) collective-permute-start(f32[512]{0:T(512)S(1)} %multiply_add_fusion.25), channel_id=1, source_target_pairs={{8,0},{16,8},{24,16},{32,24},{40,32},{48,40},{56,48},{64,56},{72,6... | collective-permute-start | bytes 6152 | tf_op jit(solution)/shard_map/ppermute | solution.py:14
  426.1 8.8 %collective-permute-start.16 = (f32[512]{0:T(512)S(1)}, f32[512]{0:T(512)S(1)}, u32[]{:S(2)}, u32[]{:S(2)}) collective-permute-start(f32[512]{0:T(512)S(1)} %multiply_add_fusion.24), channel_id=1, source_target_pairs={{8,0},{16,8},{24,16},{32,24},{40,32},{48,40},{56,48},{64,56},{72,6... | collective-permute-start | bytes 6152 | tf_op jit(solution)/shard_map/ppermute | solution.py:14
  434.9 8.8 %collective-permute-start.17 = (f32[512]{0:T(512)S(1)}, f32[512]{0:T(512)S(1)}, u32[]{:S(2)}, u32[]{:S(2)}) collective-permute-start(f32[512]{0:T(512)S(1)} %multiply_add_fusion.23), channel_id=1, source_target_pairs={{8,0},{16,8},{24,16},{32,24},{40,32},{48,40},{56,48},{64,56},{72,6... | collective-permute-start | bytes 6152 | tf_op jit(solution)/shard_map/ppermute | solution.py:14
  443.7 8.8 %collective-permute-start.18 = (f32[512]{0:T(512)S(1)}, f32[512]{0:T(512)S(1)}, u32[]{:S(2)}, u32[]{:S(2)}) collective-permute-start(f32[512]{0:T(512)S(1)} %multiply_add_fusion.22), channel_id=1, source_target_pairs={{8,0},{16,8},{24,16},{32,24},{40,32},{48,40},{56,48},{64,56},{72,6... | collective-permute-start | bytes 6152 | tf_op jit(solution)/shard_map/ppermute | solution.py:14
  452.5 8.8 %collective-permute-start.19 = (f32[512]{0:T(512)S(1)}, f32[512]{0:T(512)S(1)}, u32[]{:S(2)}, u32[]{:S(2)}) collective-permute-start(f32[512]{0:T(512)S(1)} %multiply_add_fusion.21), channel_id=1, source_target_pairs={{8,0},{16,8},{24,16},{32,24},{40,32},{48,40},{56,48},{64,56},{72,6... | collective-permute-start | bytes 6152 | tf_op jit(solution)/shard_map/ppermute | solution.py:14
  461.3 8.8 %collective-permute-start.20 = (f32[512]{0:T(512)S(1)}, f32[512]{0:T(512)S(1)}, u32[]{:S(2)}, u32[]{:S(2)}) collective-permute-start(f32[512]{0:T(512)S(1)} %multiply_add_fusion.20), channel_id=1, source_target_pairs={{8,0},{16,8},{24,16},{32,24},{40,32},{48,40},{56,48},{64,56},{72,6... | collective-permute-start | bytes 6152 | tf_op jit(solution)/shard_map/ppermute | solution.py:14
  470.1 8.8 %collective-permute-start.21 = (f32[512]{0:T(512)S(1)}, f32[512]{0:T(512)S(1)}, u32[]{:S(2)}, u32[]{:S(2)}) collective-permute-start(f32[512]{0:T(512)S(1)} %multiply_add_fusion.19), channel_id=1, source_target_pairs={{8,0},{16,8},{24,16},{32,24},{40,32},{48,40},{56,48},{64,56},{72,6... | collective-permute-start | bytes 6152 | tf_op jit(solution)/shard_map/ppermute | solution.py:14
  478.9 8.8 %collective-permute-start.22 = (f32[512]{0:T(512)S(1)}, f32[512]{0:T(512)S(1)}, u32[]{:S(2)}, u32[]{:S(2)}) collective-permute-start(f32[512]{0:T(512)S(1)} %multiply_add_fusion.18), channel_id=1, source_target_pairs={{8,0},{16,8},{24,16},{32,24},{40,32},{48,40},{56,48},{64,56},{72,6... | collective-permute-start | bytes 6152 | tf_op jit(solution)/shard_map/ppermute | solution.py:14
  487.7 8.8 %collective-permute-start.23 = (f32[512]{0:T(512)S(1)}, f32[512]{0:T(512)S(1)}, u32[]{:S(2)}, u32[]{:S(2)}) collective-permute-start(f32[512]{0:T(512)S(1)} %multiply_add_fusion.17), channel_id=1, source_target_pairs={{8,0},{16,8},{24,16},{32,24},{40,32},{48,40},{56,48},{64,56},{72,6... | collective-permute-start | bytes 6152 | tf_op jit(solution)/shard_map/ppermute | solution.py:14
  496.5 8.8 %collective-permute-start.24 = (f32[512]{0:T(512)S(1)}, f32[512]{0:T(512)S(1)}, u32[]{:S(2)}, u32[]{:S(2)}) collective-permute-start(f32[512]{0:T(512)S(1)} %multiply_add_fusion.16), channel_id=1, source_target_pairs={{8,0},{16,8},{24,16},{32,24},{40,32},{48,40},{56,48},{64,56},{72,6... | collective-permute-start | bytes 6152 | tf_op jit(solution)/shard_map/ppermute | solution.py:14
  505.3 8.8 %collective-permute-start.25 = (f32[512]{0:T(512)S(1)}, f32[512]{0:T(512)S(1)}, u32[]{:S(2)}, u32[]{:S(2)}) collective-permute-start(f32[512]{0:T(512)S(1)} %multiply_add_fusion.15), channel_id=1, source_target_pairs={{8,0},{16,8},{24,16},{32,24},{40,32},{48,40},{56,48},{64,56},{72,6... | collective-permute-start | bytes 6152 | tf_op jit(solution)/shard_map/ppermute | solution.py:14
  514.1 8.8 %collective-permute-start.26 = (f32[512]{0:T(512)S(1)}, f32[512]{0:T(512)S(1)}, u32[]{:S(2)}, u32[]{:S(2)}) collective-permute-start(f32[512]{0:T(512)S(1)} %multiply_add_fusion.14), channel_id=1, source_target_pairs={{8,0},{16,8},{24,16},{32,24},{40,32},{48,40},{56,48},{64,56},{72,6... | collective-permute-start | bytes 6152 | tf_op jit(solution)/shard_map/ppermute | solution.py:14
  522.9 8.8 %collective-permute-start.27 = (f32[512]{0:T(512)S(1)}, f32[512]{0:T(512)S(1)}, u32[]{:S(2)}, u32[]{:S(2)}) collective-permute-start(f32[512]{0:T(512)S(1)} %multiply_add_fusion.13), channel_id=1, source_target_pairs={{8,0},{16,8},{24,16},{32,24},{40,32},{48,40},{56,48},{64,56},{72,6... | collective-permute-start | bytes 6152 | tf_op jit(solution)/shard_map/ppermute | solution.py:14
  531.7 8.8 %collective-permute-start.28 = (f32[512]{0:T(512)S(1)}, f32[512]{0:T(512)S(1)}, u32[]{:S(2)}, u32[]{:S(2)}) collective-permute-start(f32[512]{0:T(512)S(1)} %multiply_add_fusion.12), channel_id=1, source_target_pairs={{8,0},{16,8},{24,16},{32,24},{40,32},{48,40},{56,48},{64,56},{72,6... | collective-permute-start | bytes 6152 | tf_op jit(solution)/shard_map/ppermute | solution.py:14
  540.4 8.8 %collective-permute-start.29 = (f32[512]{0:T(512)S(1)}, f32[512]{0:T(512)S(1)}, u32[]{:S(2)}, u32[]{:S(2)}) collective-permute-start(f32[512]{0:T(512)S(1)} %multiply_add_fusion.11), channel_id=1, source_target_pairs={{8,0},{16,8},{24,16},{32,24},{40,32},{48,40},{56,48},{64,56},{72,6... | collective-permute-start | bytes 6152 | tf_op jit(solution)/shard_map/ppermute | solution.py:14
  549.2 23.2 %collective-permute-start.30 = (f32[512]{0:T(512)S(1)}, f32[512]{0:T(512)S(1)}, u32[]{:S(2)}, u32[]{:S(2)}) collective-permute-start(f32[512]{0:T(512)S(1)} %multiply_add_fusion.10), channel_id=1, source_target_pairs={{8,0},{16,8},{24,16},{32,24},{40,32},{48,40},{56,48},{64,56},{72,6... | collective-permute-start | bytes 6152 | tf_op jit(solution)/shard_map/ppermute | solution.py:14
  558.6 16.3 %copy-start.1 = (bf16[512,512]{1,0:T(8,128)(2,1)S(1)}, bf16[512,512]{1,0:T(8,128)(2,1)}, u32[]{:S(2)}) copy-start(bf16[512,512]{1,0:T(8,128)(2,1)} %param.7) | copy-start | bytes 1572868
Sparse Core Ops, SparseCore 0:
  186.8 68.0 all-reduce.37
where the time goes:
time: 588 us; the launch traced here: 582 us
  starting transfers between devices  229 us (39%)
  blocking collectives  144 us (24%)
  waiting for transfers between devices  102 us (17%)
  local copies, waits for them, and re-layouts  47.5 us (8%)
  other arithmetic  30.2 us (5%)
  between operations  15.2 us (3%)
  matrix products  14 us (2%)
    ppermute x31, starting transfers between devices, from_behind(): return lax.ppermute(block, axis, route)  229 us
    pmax x1, blocking collectives, body(): peak_value = lax.pmax(jnp.max(failure_index, axis=0), 'tm')  73 us
    psum x1, blocking collectives, body(): mass_total = lax.psum(jnp.sum(scaled_exp, axis=0), 'tm')  70.8 us
    psum x1, waiting for transfers between devices, body(): load_rows = lax.psum(local_loads, 'elem')  63 us
    ppermute x31, waiting for transfers between devices, from_behind(): return lax.ppermute(block, axis, route)  38.6 us
    slice x66, local copies, waits for them, and re-layouts, chain_back(): lax.associative_scan(compose, (decay_rows, load_rows), reverse=True, axis...  24.4 us
    rev x2, local copies, waits for them, and re-layouts, chain_back(): lax.associative_scan(compose, (decay_rows, load_rows), reverse=True, axis...  12 us
  transfers between devices with their start and end apart: 32, of which 31 were waited for; matrix products, arithmetic and copies ran while one was open for 4% of the time, Pallas kernels for 0%

commit v1 on v0

--- a/solution.py
+++ b/solution.py
@@ -74,7 +74,9 @@
     failure_index, slopes = failure_terms(stress, col_coefs)
     peak_value = lax.pmax(jnp.max(failure_index, axis=0), "tm")
     scaled_exp = jnp.exp(sharpness * (failure_index - peak_value[None, :]))
-    mass_total = lax.psum(jnp.sum(scaled_exp, axis=0), "tm")
+    x = jnp.sum(scaled_exp, axis=0)
+    pieces = lax.all_gather(x, "tm")
+    mass_total = jnp.sum(pieces, axis=0)
     column_ks = peak_value + jnp.log(mass_total) / sharpness
     weight = sharpness * scaled_exp / mass_total[None, :]
     sensitivity = jnp.stack([weight * slopes[0], weight * slopes[1], weight * slopes[2]]).astype(

time: 588 us -> 564 us (0.959)
  blocking collectives: 144 us -> 119 us
    psum x1 -> x0, blocking collectives: 70.8 us -> none  [body(): mass_total = lax.psum(jnp.sum(scaled_exp, axis=0), 'tm')]
    all_gather x0 -> x1, blocking collectives: none -> 45.8 us  [body(): pieces = lax.all_gather(x, 'tm')]
where the time goes in v1:
time: 564 us; the launch traced here: 558 us
  starting transfers between devices  230 us (41%)
  blocking collectives  119 us (21%)
  waiting for transfers between devices  103 us (18%)
  local copies, waits for them, and re-layouts  47.3 us (8%)
  other arithmetic  30.5 us (5%)
  between operations  15.2 us (3%)
  matrix products  14 us (2%)
    ppermute x31, starting transfers between devices, from_behind(): return lax.ppermute(block, axis, route)  230 us
    pmax x1, blocking collectives, body(): peak_value = lax.pmax(jnp.max(failure_index, axis=0), 'tm')  73 us
    psum x1, waiting for transfers between devices, body(): load_rows = lax.psum(local_loads, 'elem')  64.3 us
    all_gather x1, blocking collectives, body(): pieces = lax.all_gather(x, 'tm')  45.8 us
    ppermute x31, waiting for transfers between devices, from_behind(): return lax.ppermute(block, axis, route)  38.4 us
    slice x66, local copies, waits for them, and re-layouts, chain_back(): lax.associative_scan(compose, (decay_rows, load_rows), reverse=True, axis...  24.4 us
    rev x2, local copies, waits for them, and re-layouts, chain_back(): lax.associative_scan(compose, (decay_rows, load_rows), reverse=True, axis...  12 us
    another operation x2, other arithmetic  11.7 us
  transfers between devices with their start and end apart: 32, of which 31 were waited for; matrix products, arithmetic and copies ran while one was open for 4% of the time, Pallas kernels for 0%

profile of v1, /device:TPU:128, one launch (start us, length us, event | category | flops | bytes accessed | tf_op | source)
XLA Modules:
  0.0 558.1 jit_solution(3512406175308989790)
XLA Ops:
  8.4 5.5 convolution_bitcast_fusion
  13.9 4.3 fusion.46
  18.3 1.5 copy-done.2
  19.7 73.0 %pmax.7 = f32[2048]{0:T(1024)S(1)} all-reduce(f32[2048]{0:T(1024)S(1)} %get-tuple-element.4), channel_id=1, replica_groups=mesh['tm'=32,'elem'=8] {'tm'}, use_global_device_ids=true, to_apply=%region_1.0 | all-reduce | flops 2048 | bytes 16384 | tf_op jit(solution)/shard_map/pmax | solution.py:75
  92.7 2.9 exponential_reduce_fusion
  95.6 45.8 %all-gather = f32[65536]{0:T(1024)S(1)} all-gather(f32[2048]{0:T(1024)S(1)} %exponential_reduce_fusion), channel_id=2, replica_groups=mesh['tm'=32,'elem'=8] {'tm'}, dimensions={0}, use_global_device_ids=true | all-gather | bytes 270336 | tf_op jit(solution)/shard_map/all_gather | solution.py:78
  141.6 8.0 %multiply_convert_fusion.2 = (bf16[1,512,2048]{2,1,0:T(8,128)(2,1)}, f32[1,512,2048]{2,1,0:T(8,128)S(1)}) fusion(f32[3,512,2048]{2,1,0:T(8,128)} %copy-done.2, f32[2048]{0:T(1024)S(1)} %bitcast.140, f32[2048]{0:T(1024)S(1)} %bitcast.123, f32[2048]{0:T(1024)S(1)} %bitcast.135, f32[2048]{0:T(1024)S(1)} %reduce_sum.19, f32[2048]{0:T(1024)S(1)} %pmax.7, ...), kind=kLoop, calls=%fused_computation.34 | loop fusion | flops 27262976 | bytes 18956288 | tf_op jit(solution)/shard_map/convert
  150.5 3.7 multiply_convert_fusion.1
  154.2 7.5 %fusion.21 = f32[512,512]{1,0:T(8,128)} fusion(bf16[3,512,2048]{2,1,0:T(8,128)(2,1)S(1)} %bitcast.58, bf16[1,512,2048]{2,1,0:T(8,128)(2,1)} %get-tuple-element.7, bf16[1,512,2048]{2,1,0:T(8,128)(2,1)} %get-tuple-element.6, bf16[1,512,2048]{2,1,0:T(8,128)(2,1)} %get-tuple-element.2), kind=kOutput, calls=%fused_computation.36 | convolution fusion | flops 3227516928 | bytes 13631488 | tf_op jit(solution)/shard_map/dot_general | solution.py:85
  164.0 2.9 slice.328
  166.9 64.3 %all-reduce.38.cloned.1.call-done = f32[512,512]{1,0:T(8,128)} async-done(((f32[512,512]{1,0:T(8,128)}), f32[512,512]{1,0:T(8,128)}) %all-reduce.38.cloned.1.call-update) | async-done | bytes 1048592 | tf_op jit(solution)/shard_map/psum | solution.py:88
  231.2 3.0 slice.329
  234.5 3.0 slice.333
  244.0 3.7 slice.325
  247.6 4.9 slice.326
  253.4 2.3 add_multiply_fusion
  255.9 4.6 pad.127
  261.4 2.7 pad.126
  264.8 4.5 collective-permute-start
  269.3 1.3 collective-permute-done
  270.6 7.5 %collective-permute-start.1 = (f32[512]{0:T(512)S(1)}, f32[512]{0:T(512)S(1)}, u32[]{:S(2)}, u32[]{:S(2)}) collective-permute-start(f32[512]{0:T(512)S(1)} %multiply_add_fusion.39), channel_id=1, source_target_pairs={{8,0},{16,8},{24,16},{32,24},{40,32},{48,40},{56,48},{64,56},{72,6... | collective-permute-start | bytes 6152 | tf_op jit(solution)/shard_map/ppermute | solution.py:14
  278.1 1.3 collective-permute-done.1
  279.4 7.5 %collective-permute-start.2 = (f32[512]{0:T(512)S(1)}, f32[512]{0:T(512)S(1)}, u32[]{:S(2)}, u32[]{:S(2)}) collective-permute-start(f32[512]{0:T(512)S(1)} %multiply_add_fusion.38), channel_id=1, source_target_pairs={{8,0},{16,8},{24,16},{32,24},{40,32},{48,40},{56,48},{64,56},{72,6... | collective-permute-start | bytes 6152 | tf_op jit(solution)/shard_map/ppermute | solution.py:14
  286.9 1.3 collective-permute-done.2
  288.2 7.5 %collective-permute-start.3 = (f32[512]{0:T(512)S(1)}, f32[512]{0:T(512)S(1)}, u32[]{:S(2)}, u32[]{:S(2)}) collective-permute-start(f32[512]{0:T(512)S(1)} %multiply_add_fusion.37), channel_id=1, source_target_pairs={{8,0},{16,8},{24,16},{32,24},{40,32},{48,40},{56,48},{64,56},{72,6... | collective-permute-start | bytes 6152 | tf_op jit(solution)/shard_map/ppermute | solution.py:14
  295.7 1.3 collective-permute-done.3
  297.0 7.5 %collective-permute-start.4 = (f32[512]{0:T(512)S(1)}, f32[512]{0:T(512)S(1)}, u32[]{:S(2)}, u32[]{:S(2)}) collective-permute-start(f32[512]{0:T(512)S(1)} %multiply_add_fusion.36), channel_id=1, source_target_pairs={{8,0},{16,8},{24,16},{32,24},{40,32},{48,40},{56,48},{64,56},{72,6... | collective-permute-start | bytes 6152 | tf_op jit(solution)/shard_map/ppermute | solution.py:14
  304.5 1.3 collective-permute-done.4
  305.8 7.7 %collective-permute-start.5 = (f32[512]{0:T(512)S(1)}, f32[512]{0:T(512)S(1)}, u32[]{:S(2)}, u32[]{:S(2)}) collective-permute-start(f32[512]{0:T(512)S(1)} %multiply_add_fusion.35), channel_id=1, source_target_pairs={{8,0},{16,8},{24,16},{32,24},{40,32},{48,40},{56,48},{64,56},{72,6... | collective-permute-start | bytes 6152 | tf_op jit(solution)/shard_map/ppermute | solution.py:14
  314.6 7.5 %collective-permute-start.6 = (f32[512]{0:T(512)S(1)}, f32[512]{0:T(512)S(1)}, u32[]{:S(2)}, u32[]{:S(2)}) collective-permute-start(f32[512]{0:T(512)S(1)} %multiply_add_fusion.34), channel_id=1, source_target_pairs={{8,0},{16,8},{24,16},{32,24},{40,32},{48,40},{56,48},{64,56},{72,6... | collective-permute-start | bytes 6152 | tf_op jit(solution)/shard_map/ppermute | solution.py:14
  322.1 1.3 collective-permute-done.6
  323.4 7.5 %collective-permute-start.7 = (f32[512]{0:T(512)S(1)}, f32[512]{0:T(512)S(1)}, u32[]{:S(2)}, u32[]{:S(2)}) collective-permute-start(f32[512]{0:T(512)S(1)} %multiply_add_fusion.33), channel_id=1, source_target_pairs={{8,0},{16,8},{24,16},{32,24},{40,32},{48,40},{56,48},{64,56},{72,6... | collective-permute-start | bytes 6152 | tf_op jit(solution)/shard_map/ppermute | solution.py:14
  330.9 1.3 collective-permute-done.7
  332.2 7.5 %collective-permute-start.8 = (f32[512]{0:T(512)S(1)}, f32[512]{0:T(512)S(1)}, u32[]{:S(2)}, u32[]{:S(2)}) collective-permute-start(f32[512]{0:T(512)S(1)} %multiply_add_fusion.32), channel_id=1, source_target_pairs={{8,0},{16,8},{24,16},{32,24},{40,32},{48,40},{56,48},{64,56},{72,6... | collective-permute-start | bytes 6152 | tf_op jit(solution)/shard_map/ppermute | solution.py:14
  339.7 1.3 collective-permute-done.8
  341.0 7.5 %collective-permute-start.9 = (f32[512]{0:T(512)S(1)}, f32[512]{0:T(512)S(1)}, u32[]{:S(2)}, u32[]{:S(2)}) collective-permute-start(f32[512]{0:T(512)S(1)} %multiply_add_fusion.31), channel_id=1, source_target_pairs={{8,0},{16,8},{24,16},{32,24},{40,32},{48,40},{56,48},{64,56},{72,6... | collective-permute-start | bytes 6152 | tf_op jit(solution)/shard_map/ppermute | solution.py:14
  348.5 1.3 collective-permute-done.9
  349.8 7.5 %collective-permute-start.10 = (f32[512]{0:T(512)S(1)}, f32[512]{0:T(512)S(1)}, u32[]{:S(2)}, u32[]{:S(2)}) collective-permute-start(f32[512]{0:T(512)S(1)} %multiply_add_fusion.30), channel_id=1, source_target_pairs={{8,0},{16,8},{24,16},{32,24},{40,32},{48,40},{56,48},{64,56},{72,6... | collective-permute-start | bytes 6152 | tf_op jit(solution)/shard_map/ppermute | solution.py:14
  358.5 7.5 %collective-permute-start.11 = (f32[512]{0:T(512)S(1)}, f32[512]{0:T(512)S(1)}, u32[]{:S(2)}, u32[]{:S(2)}) collective-permute-start(f32[512]{0:T(512)S(1)} %multiply_add_fusion.29), channel_id=1, source_target_pairs={{8,0},{16,8},{24,16},{32,24},{40,32},{48,40},{56,48},{64,56},{72,6... | collective-permute-start | bytes 6152 | tf_op jit(solution)/shard_map/ppermute | solution.py:14
  367.3 7.5 %collective-permute-start.12 = (f32[512]{0:T(512)S(1)}, f32[512]{0:T(512)S(1)}, u32[]{:S(2)}, u32[]{:S(2)}) collective-permute-start(f32[512]{0:T(512)S(1)} %multiply_add_fusion.28), channel_id=1, source_target_pairs={{8,0},{16,8},{24,16},{32,24},{40,32},{48,40},{56,48},{64,56},{72,6... | collective-permute-start | bytes 6152 | tf_op jit(solution)/shard_map/ppermute | solution.py:14
  376.1 7.5 %collective-permute-start.13 = (f32[512]{0:T(512)S(1)}, f32[512]{0:T(512)S(1)}, u32[]{:S(2)}, u32[]{:S(2)}) collective-permute-start(f32[512]{0:T(512)S(1)} %multiply_add_fusion.27), channel_id=1, source_target_pairs={{8,0},{16,8},{24,16},{32,24},{40,32},{48,40},{56,48},{64,56},{72,6... | collective-permute-start | bytes 6152 | tf_op jit(solution)/shard_map/ppermute | solution.py:14
  384.9 7.5 %collective-permute-start.14 = (f32[512]{0:T(512)S(1)}, f32[512]{0:T(512)S(1)}, u32[]{:S(2)}, u32[]{:S(2)}) collective-permute-start(f32[512]{0:T(512)S(1)} %multiply_add_fusion.26), channel_id=1, source_target_pairs={{8,0},{16,8},{24,16},{32,24},{40,32},{48,40},{56,48},{64,56},{72,6... | collective-permute-start | bytes 6152 | tf_op jit(solution)/shard_map/ppermute | solution.py:14
  392.4 1.3 collective-permute-done.14
  393.7 7.5 %collective-permute-start.15 = (f32[512]{0:T(512)S(1)}, f32[512]{0:T(512)S(1)}, u32[]{:S(2)}, u32[]{:S(2)}) collective-permute-start(f32[512]{0:T(512)S(1)} %multiply_add_fusion.25), channel_id=1, source_target_pairs={{8,0},{16,8},{24,16},{32,24},{40,32},{48,40},{56,48},{64,56},{72,6... | collective-permute-start | bytes 6152 | tf_op jit(solution)/shard_map/ppermute | solution.py:14
  402.5 7.5 %collective-permute-start.16 = (f32[512]{0:T(512)S(1)}, f32[512]{0:T(512)S(1)}, u32[]{:S(2)}, u32[]{:S(2)}) collective-permute-start(f32[512]{0:T(512)S(1)} %multiply_add_fusion.24), channel_id=1, source_target_pairs={{8,0},{16,8},{24,16},{32,24},{40,32},{48,40},{56,48},{64,56},{72,6... | collective-permute-start | bytes 6152 | tf_op jit(solution)/shard_map/ppermute | solution.py:14
  411.3 7.5 %collective-permute-start.17 = (f32[512]{0:T(512)S(1)}, f32[512]{0:T(512)S(1)}, u32[]{:S(2)}, u32[]{:S(2)}) collective-permute-start(f32[512]{0:T(512)S(1)} %multiply_add_fusion.23), channel_id=1, source_target_pairs={{8,0},{16,8},{24,16},{32,24},{40,32},{48,40},{56,48},{64,56},{72,6... | collective-permute-start | bytes 6152 | tf_op jit(solution)/shard_map/ppermute | solution.py:14
  420.1 7.5 %collective-permute-start.18 = (f32[512]{0:T(512)S(1)}, f32[512]{0:T(512)S(1)}, u32[]{:S(2)}, u32[]{:S(2)}) collective-permute-start(f32[512]{0:T(512)S(1)} %multiply_add_fusion.22), channel_id=1, source_target_pairs={{8,0},{16,8},{24,16},{32,24},{40,32},{48,40},{56,48},{64,56},{72,6... | collective-permute-start | bytes 6152 | tf_op jit(solution)/shard_map/ppermute | solution.py:14
  428.9 7.5 %collective-permute-start.19 = (f32[512]{0:T(512)S(1)}, f32[512]{0:T(512)S(1)}, u32[]{:S(2)}, u32[]{:S(2)}) collective-permute-start(f32[512]{0:T(512)S(1)} %multiply_add_fusion.21), channel_id=1, source_target_pairs={{8,0},{16,8},{24,16},{32,24},{40,32},{48,40},{56,48},{64,56},{72,6... | collective-permute-start | bytes 6152 | tf_op jit(solution)/shard_map/ppermute | solution.py:14
  437.7 7.5 %collective-permute-start.20 = (f32[512]{0:T(512)S(1)}, f32[512]{0:T(512)S(1)}, u32[]{:S(2)}, u32[]{:S(2)}) collective-permute-start(f32[512]{0:T(512)S(1)} %multiply_add_fusion.20), channel_id=1, source_target_pairs={{8,0},{16,8},{24,16},{32,24},{40,32},{48,40},{56,48},{64,56},{72,6... | collective-permute-start | bytes 6152 | tf_op jit(solution)/shard_map/ppermute | solution.py:14
  446.5 7.5 %collective-permute-start.21 = (f32[512]{0:T(512)S(1)}, f32[512]{0:T(512)S(1)}, u32[]{:S(2)}, u32[]{:S(2)}) collective-permute-start(f32[512]{0:T(512)S(1)} %multiply_add_fusion.19), channel_id=1, source_target_pairs={{8,0},{16,8},{24,16},{32,24},{40,32},{48,40},{56,48},{64,56},{72,6... | collective-permute-start | bytes 6152 | tf_op jit(solution)/shard_map/ppermute | solution.py:14
  454.0 1.3 collective-permute-done.21
  455.3 7.5 %collective-permute-start.22 = (f32[512]{0:T(512)S(1)}, f32[512]{0:T(512)S(1)}, u32[]{:S(2)}, u32[]{:S(2)}) collective-permute-start(f32[512]{0:T(512)S(1)} %multiply_add_fusion.18), channel_id=1, source_target_pairs={{8,0},{16,8},{24,16},{32,24},{40,32},{48,40},{56,48},{64,56},{72,6... | collective-permute-start | bytes 6152 | tf_op jit(solution)/shard_map/ppermute | solution.py:14
  464.1 7.5 %collective-permute-start.23 = (f32[512]{0:T(512)S(1)}, f32[512]{0:T(512)S(1)}, u32[]{:S(2)}, u32[]{:S(2)}) collective-permute-start(f32[512]{0:T(512)S(1)} %multiply_add_fusion.17), channel_id=1, source_target_pairs={{8,0},{16,8},{24,16},{32,24},{40,32},{48,40},{56,48},{64,56},{72,6... | collective-permute-start | bytes 6152 | tf_op jit(solution)/shard_map/ppermute | solution.py:14
  472.8 7.5 %collective-permute-start.24 = (f32[512]{0:T(512)S(1)}, f32[512]{0:T(512)S(1)}, u32[]{:S(2)}, u32[]{:S(2)}) collective-permute-start(f32[512]{0:T(512)S(1)} %multiply_add_fusion.16), channel_id=1, source_target_pairs={{8,0},{16,8},{24,16},{32,24},{40,32},{48,40},{56,48},{64,56},{72,6... | collective-permute-start | bytes 6152 | tf_op jit(solution)/shard_map/ppermute | solution.py:14
  481.6 7.5 %collective-permute-start.25 = (f32[512]{0:T(512)S(1)}, f32[512]{0:T(512)S(1)}, u32[]{:S(2)}, u32[]{:S(2)}) collective-permute-start(f32[512]{0:T(512)S(1)} %multiply_add_fusion.15), channel_id=1, source_target_pairs={{8,0},{16,8},{24,16},{32,24},{40,32},{48,40},{56,48},{64,56},{72,6... | collective-permute-start | bytes 6152 | tf_op jit(solution)/shard_map/ppermute | solution.py:14
  490.4 7.5 %collective-permute-start.26 = (f32[512]{0:T(512)S(1)}, f32[512]{0:T(512)S(1)}, u32[]{:S(2)}, u32[]{:S(2)}) collective-permute-start(f32[512]{0:T(512)S(1)} %multiply_add_fusion.14), channel_id=1, source_target_pairs={{8,0},{16,8},{24,16},{32,24},{40,32},{48,40},{56,48},{64,56},{72,6... | collective-permute-start | bytes 6152 | tf_op jit(solution)/shard_map/ppermute | solution.py:14
  499.2 7.5 %collective-permute-start.27 = (f32[512]{0:T(512)S(1)}, f32[512]{0:T(512)S(1)}, u32[]{:S(2)}, u32[]{:S(2)}) collective-permute-start(f32[512]{0:T(512)S(1)} %multiply_add_fusion.13), channel_id=1, source_target_pairs={{8,0},{16,8},{24,16},{32,24},{40,32},{48,40},{56,48},{64,56},{72,6... | collective-permute-start | bytes 6152 | tf_op jit(solution)/shard_map/ppermute | solution.py:14
  508.0 7.5 %collective-permute-start.28 = (f32[512]{0:T(512)S(1)}, f32[512]{0:T(512)S(1)}, u32[]{:S(2)}, u32[]{:S(2)}) collective-permute-start(f32[512]{0:T(512)S(1)} %multiply_add_fusion.12), channel_id=1, source_target_pairs={{8,0},{16,8},{24,16},{32,24},{40,32},{48,40},{56,48},{64,56},{72,6... | collective-permute-start | bytes 6152 | tf_op jit(solution)/shard_map/ppermute | solution.py:14
  516.8 7.5 %collective-permute-start.29 = (f32[512]{0:T(512)S(1)}, f32[512]{0:T(512)S(1)}, u32[]{:S(2)}, u32[]{:S(2)}) collective-permute-start(f32[512]{0:T(512)S(1)} %multiply_add_fusion.11), channel_id=1, source_target_pairs={{8,0},{16,8},{24,16},{32,24},{40,32},{48,40},{56,48},{64,56},{72,6... | collective-permute-start | bytes 6152 | tf_op jit(solution)/shard_map/ppermute | solution.py:14
  525.6 7.5 %collective-permute-start.30 = (f32[512]{0:T(512)S(1)}, f32[512]{0:T(512)S(1)}, u32[]{:S(2)}, u32[]{:S(2)}) collective-permute-start(f32[512]{0:T(512)S(1)} %multiply_add_fusion.10), channel_id=1, source_target_pairs={{8,0},{16,8},{24,16},{32,24},{40,32},{48,40},{56,48},{64,56},{72,6... | collective-permute-start | bytes 6152 | tf_op jit(solution)/shard_map/ppermute | solution.py:14
  534.9 1.8 add.402
  536.7 6.9 %rev.9 = f32[512,512]{1,0:T(8,128)S(1)} reverse(f32[512,512]{1,0:T(8,128)} %add.411), dimensions={0} | reverse | bytes 2097152 | tf_op jit(solution)/shard_map/rev | solution.py:58
  543.6 5.2 rev.8
  548.8 2.4 multiply_add_fusion
  (216 shorter events, 39.2 us)
Async XLA Ops:
  7.2 1.2 copy-start
  7.2 224.1 %all-reduce.38.cloned.1.call-start = ((), (), s32[]{:S(2)}) async-start(), calls=%async_computation | async-start | bytes 2097152 | tf_op jit(solution)/shard_map/psum | solution.py:88
  13.9 5.8 %copy-start.2 = (f32[3,512,2048]{2,1,0:T(8,128)}, f32[3,512,2048]{2,1,0:T(8,128)S(1)}, u32[]{:S(2)}) copy-start(f32[3,512,2048]{2,1,0:T(8,128)S(1)} %convolution_bitcast_fusion) | copy-start | bytes 37748740
  141.5 9.0 %copy-start.3 = (f32[3,512,2048]{2,1,0:T(8,128)S(1)}, f32[3,512,2048]{2,1,0:T(8,128)}, u32[]{:S(2)}) copy-start(f32[3,512,2048]{2,1,0:T(8,128)} %copy-done.2) | copy-start | bytes 37748740
  141.5 12.7 %slice-start = ((s8[6291456]{0:T(1024)(128)(4,1)}), s8[4194304]{0:T(1024)(128)(4,1)S(1)}, s32[]{:S(2)}) async-start(s8[6291456]{0:T(1024)(128)(4,1)} %bitcast.57), calls=%async_computation.1 | async-start | bytes 8388608
  150.5 3.7 slice-start.1
  154.2 7.5 %copy-start.4 = (f32[512,512]{1,0:T(8,128)S(1)}, f32[512,512]{1,0:T(8,128)}, u32[]{:S(2)}) copy-start(f32[512,512]{1,0:T(8,128)} %param.9) | copy-start | bytes 3145732
  255.7 5.6 copy-start.5
  264.8 5.8 %collective-permute-start = (f32[512]{0:T(512)S(1)}, f32[512]{0:T(512)S(1)}, u32[]{:S(2)}, u32[]{:S(2)}) collective-permute-start(f32[512]{0:T(512)S(1)} %multiply_add_fusion.40), channel_id=1, source_target_pairs={{8,0},{16,8},{24,16},{32,24},{40,32},{48,40},{56,48},{64,56},{72,6... | collective-permute-start | bytes 6152 | tf_op jit(solution)/shard_map/ppermute | solution.py:14
  270.6 8.8 %collective-permute-start.1 = (f32[512]{0:T(512)S(1)}, f32[512]{0:T(512)S(1)}, u32[]{:S(2)}, u32[]{:S(2)}) collective-permute-start(f32[512]{0:T(512)S(1)} %multiply_add_fusion.39), channel_id=1, source_target_pairs={{8,0},{16,8},{24,16},{32,24},{40,32},{48,40},{56,48},{64,56},{72,6... | collective-permute-start | bytes 6152 | tf_op jit(solution)/shard_map/ppermute | solution.py:14
  279.4 8.8 %collective-permute-start.2 = (f32[512]{0:T(512)S(1)}, f32[512]{0:T(512)S(1)}, u32[]{:S(2)}, u32[]{:S(2)}) collective-permute-start(f32[512]{0:T(512)S(1)} %multiply_add_fusion.38), channel_id=1, source_target_pairs={{8,0},{16,8},{24,16},{32,24},{40,32},{48,40},{56,48},{64,56},{72,6... | collective-permute-start | bytes 6152 | tf_op jit(solution)/shard_map/ppermute | solution.py:14
  288.2 8.8 %collective-permute-start.3 = (f32[512]{0:T(512)S(1)}, f32[512]{0:T(512)S(1)}, u32[]{:S(2)}, u32[]{:S(2)}) collective-permute-start(f32[512]{0:T(512)S(1)} %multiply_add_fusion.37), channel_id=1, source_target_pairs={{8,0},{16,8},{24,16},{32,24},{40,32},{48,40},{56,48},{64,56},{72,6... | collective-permute-start | bytes 6152 | tf_op jit(solution)/shard_map/ppermute | solution.py:14
  297.0 8.8 %collective-permute-start.4 = (f32[512]{0:T(512)S(1)}, f32[512]{0:T(512)S(1)}, u32[]{:S(2)}, u32[]{:S(2)}) collective-permute-start(f32[512]{0:T(512)S(1)} %multiply_add_fusion.36), channel_id=1, source_target_pairs={{8,0},{16,8},{24,16},{32,24},{40,32},{48,40},{56,48},{64,56},{72,6... | collective-permute-start | bytes 6152 | tf_op jit(solution)/shard_map/ppermute | solution.py:14
  305.8 8.8 %collective-permute-start.5 = (f32[512]{0:T(512)S(1)}, f32[512]{0:T(512)S(1)}, u32[]{:S(2)}, u32[]{:S(2)}) collective-permute-start(f32[512]{0:T(512)S(1)} %multiply_add_fusion.35), channel_id=1, source_target_pairs={{8,0},{16,8},{24,16},{32,24},{40,32},{48,40},{56,48},{64,56},{72,6... | collective-permute-start | bytes 6152 | tf_op jit(solution)/shard_map/ppermute | solution.py:14
  314.6 8.8 %collective-permute-start.6 = (f32[512]{0:T(512)S(1)}, f32[512]{0:T(512)S(1)}, u32[]{:S(2)}, u32[]{:S(2)}) collective-permute-start(f32[512]{0:T(512)S(1)} %multiply_add_fusion.34), channel_id=1, source_target_pairs={{8,0},{16,8},{24,16},{32,24},{40,32},{48,40},{56,48},{64,56},{72,6... | collective-permute-start | bytes 6152 | tf_op jit(solution)/shard_map/ppermute | solution.py:14
  323.4 8.8 %collective-permute-start.7 = (f32[512]{0:T(512)S(1)}, f32[512]{0:T(512)S(1)}, u32[]{:S(2)}, u32[]{:S(2)}) collective-permute-start(f32[512]{0:T(512)S(1)} %multiply_add_fusion.33), channel_id=1, source_target_pairs={{8,0},{16,8},{24,16},{32,24},{40,32},{48,40},{56,48},{64,56},{72,6... | collective-permute-start | bytes 6152 | tf_op jit(solution)/shard_map/ppermute | solution.py:14
  332.2 8.8 %collective-permute-start.8 = (f32[512]{0:T(512)S(1)}, f32[512]{0:T(512)S(1)}, u32[]{:S(2)}, u32[]{:S(2)}) collective-permute-start(f32[512]{0:T(512)S(1)} %multiply_add_fusion.32), channel_id=1, source_target_pairs={{8,0},{16,8},{24,16},{32,24},{40,32},{48,40},{56,48},{64,56},{72,6... | collective-permute-start | bytes 6152 | tf_op jit(solution)/shard_map/ppermute | solution.py:14
  341.0 8.8 %collective-permute-start.9 = (f32[512]{0:T(512)S(1)}, f32[512]{0:T(512)S(1)}, u32[]{:S(2)}, u32[]{:S(2)}) collective-permute-start(f32[512]{0:T(512)S(1)} %multiply_add_fusion.31), channel_id=1, source_target_pairs={{8,0},{16,8},{24,16},{32,24},{40,32},{48,40},{56,48},{64,56},{72,6... | collective-permute-start | bytes 6152 | tf_op jit(solution)/shard_map/ppermute | solution.py:14
  349.8 8.8 %collective-permute-start.10 = (f32[512]{0:T(512)S(1)}, f32[512]{0:T(512)S(1)}, u32[]{:S(2)}, u32[]{:S(2)}) collective-permute-start(f32[512]{0:T(512)S(1)} %multiply_add_fusion.30), channel_id=1, source_target_pairs={{8,0},{16,8},{24,16},{32,24},{40,32},{48,40},{56,48},{64,56},{72,6... | collective-permute-start | bytes 6152 | tf_op jit(solution)/shard_map/ppermute | solution.py:14
  358.5 8.8 %collective-permute-start.11 = (f32[512]{0:T(512)S(1)}, f32[512]{0:T(512)S(1)}, u32[]{:S(2)}, u32[]{:S(2)}) collective-permute-start(f32[512]{0:T(512)S(1)} %multiply_add_fusion.29), channel_id=1, source_target_pairs={{8,0},{16,8},{24,16},{32,24},{40,32},{48,40},{56,48},{64,56},{72,6... | collective-permute-start | bytes 6152 | tf_op jit(solution)/shard_map/ppermute | solution.py:14
  367.3 8.8 %collective-permute-start.12 = (f32[512]{0:T(512)S(1)}, f32[512]{0:T(512)S(1)}, u32[]{:S(2)}, u32[]{:S(2)}) collective-permute-start(f32[512]{0:T(512)S(1)} %multiply_add_fusion.28), channel_id=1, source_target_pairs={{8,0},{16,8},{24,16},{32,24},{40,32},{48,40},{56,48},{64,56},{72,6... | collective-permute-start | bytes 6152 | tf_op jit(solution)/shard_map/ppermute | solution.py:14
  376.1 8.8 %collective-permute-start.13 = (f32[512]{0:T(512)S(1)}, f32[512]{0:T(512)S(1)}, u32[]{:S(2)}, u32[]{:S(2)}) collective-permute-start(f32[512]{0:T(512)S(1)} %multiply_add_fusion.27), channel_id=1, source_target_pairs={{8,0},{16,8},{24,16},{32,24},{40,32},{48,40},{56,48},{64,56},{72,6... | collective-permute-start | bytes 6152 | tf_op jit(solution)/shard_map/ppermute | solution.py:14
  384.9 8.8 %collective-permute-start.14 = (f32[512]{0:T(512)S(1)}, f32[512]{0:T(512)S(1)}, u32[]{:S(2)}, u32[]{:S(2)}) collective-permute-start(f32[512]{0:T(512)S(1)} %multiply_add_fusion.26), channel_id=1, source_target_pairs={{8,0},{16,8},{24,16},{32,24},{40,32},{48,40},{56,48},{64,56},{72,6... | collective-permute-start | bytes 6152 | tf_op jit(solution)/shard_map/ppermute | solution.py:14
  393.7 8.8 %collective-permute-start.15 = (f32[512]{0:T(512)S(1)}, f32[512]{0:T(512)S(1)}, u32[]{:S(2)}, u32[]{:S(2)}) collective-permute-start(f32[512]{0:T(512)S(1)} %multiply_add_fusion.25), channel_id=1, source_target_pairs={{8,0},{16,8},{24,16},{32,24},{40,32},{48,40},{56,48},{64,56},{72,6... | collective-permute-start | bytes 6152 | tf_op jit(solution)/shard_map/ppermute | solution.py:14
  402.5 8.8 %collective-permute-start.16 = (f32[512]{0:T(512)S(1)}, f32[512]{0:T(512)S(1)}, u32[]{:S(2)}, u32[]{:S(2)}) collective-permute-start(f32[512]{0:T(512)S(1)} %multiply_add_fusion.24), channel_id=1, source_target_pairs={{8,0},{16,8},{24,16},{32,24},{40,32},{48,40},{56,48},{64,56},{72,6... | collective-permute-start | bytes 6152 | tf_op jit(solution)/shard_map/ppermute | solution.py:14
  411.3 8.8 %collective-permute-start.17 = (f32[512]{0:T(512)S(1)}, f32[512]{0:T(512)S(1)}, u32[]{:S(2)}, u32[]{:S(2)}) collective-permute-start(f32[512]{0:T(512)S(1)} %multiply_add_fusion.23), channel_id=1, source_target_pairs={{8,0},{16,8},{24,16},{32,24},{40,32},{48,40},{56,48},{64,56},{72,6... | collective-permute-start | bytes 6152 | tf_op jit(solution)/shard_map/ppermute | solution.py:14
  420.1 8.8 %collective-permute-start.18 = (f32[512]{0:T(512)S(1)}, f32[512]{0:T(512)S(1)}, u32[]{:S(2)}, u32[]{:S(2)}) collective-permute-start(f32[512]{0:T(512)S(1)} %multiply_add_fusion.22), channel_id=1, source_target_pairs={{8,0},{16,8},{24,16},{32,24},{40,32},{48,40},{56,48},{64,56},{72,6... | collective-permute-start | bytes 6152 | tf_op jit(solution)/shard_map/ppermute | solution.py:14
  428.9 8.8 %collective-permute-start.19 = (f32[512]{0:T(512)S(1)}, f32[512]{0:T(512)S(1)}, u32[]{:S(2)}, u32[]{:S(2)}) collective-permute-start(f32[512]{0:T(512)S(1)} %multiply_add_fusion.21), channel_id=1, source_target_pairs={{8,0},{16,8},{24,16},{32,24},{40,32},{48,40},{56,48},{64,56},{72,6... | collective-permute-start | bytes 6152 | tf_op jit(solution)/shard_map/ppermute | solution.py:14
  437.7 8.8 %collective-permute-start.20 = (f32[512]{0:T(512)S(1)}, f32[512]{0:T(512)S(1)}, u32[]{:S(2)}, u32[]{:S(2)}) collective-permute-start(f32[512]{0:T(512)S(1)} %multiply_add_fusion.20), channel_id=1, source_target_pairs={{8,0},{16,8},{24,16},{32,24},{40,32},{48,40},{56,48},{64,56},{72,6... | collective-permute-start | bytes 6152 | tf_op jit(solution)/shard_map/ppermute | solution.py:14
  446.5 8.8 %collective-permute-start.21 = (f32[512]{0:T(512)S(1)}, f32[512]{0:T(512)S(1)}, u32[]{:S(2)}, u32[]{:S(2)}) collective-permute-start(f32[512]{0:T(512)S(1)} %multiply_add_fusion.19), channel_id=1, source_target_pairs={{8,0},{16,8},{24,16},{32,24},{40,32},{48,40},{56,48},{64,56},{72,6... | collective-permute-start | bytes 6152 | tf_op jit(solution)/shard_map/ppermute | solution.py:14
  455.3 8.8 %collective-permute-start.22 = (f32[512]{0:T(512)S(1)}, f32[512]{0:T(512)S(1)}, u32[]{:S(2)}, u32[]{:S(2)}) collective-permute-start(f32[512]{0:T(512)S(1)} %multiply_add_fusion.18), channel_id=1, source_target_pairs={{8,0},{16,8},{24,16},{32,24},{40,32},{48,40},{56,48},{64,56},{72,6... | collective-permute-start | bytes 6152 | tf_op jit(solution)/shard_map/ppermute | solution.py:14
  464.1 8.8 %collective-permute-start.23 = (f32[512]{0:T(512)S(1)}, f32[512]{0:T(512)S(1)}, u32[]{:S(2)}, u32[]{:S(2)}) collective-permute-start(f32[512]{0:T(512)S(1)} %multiply_add_fusion.17), channel_id=1, source_target_pairs={{8,0},{16,8},{24,16},{32,24},{40,32},{48,40},{56,48},{64,56},{72,6... | collective-permute-start | bytes 6152 | tf_op jit(solution)/shard_map/ppermute | solution.py:14
  472.8 8.8 %collective-permute-start.24 = (f32[512]{0:T(512)S(1)}, f32[512]{0:T(512)S(1)}, u32[]{:S(2)}, u32[]{:S(2)}) collective-permute-start(f32[512]{0:T(512)S(1)} %multiply_add_fusion.16), channel_id=1, source_target_pairs={{8,0},{16,8},{24,16},{32,24},{40,32},{48,40},{56,48},{64,56},{72,6... | collective-permute-start | bytes 6152 | tf_op jit(solution)/shard_map/ppermute | solution.py:14
  481.6 8.8 %collective-permute-start.25 = (f32[512]{0:T(512)S(1)}, f32[512]{0:T(512)S(1)}, u32[]{:S(2)}, u32[]{:S(2)}) collective-permute-start(f32[512]{0:T(512)S(1)} %multiply_add_fusion.15), channel_id=1, source_target_pairs={{8,0},{16,8},{24,16},{32,24},{40,32},{48,40},{56,48},{64,56},{72,6... | collective-permute-start | bytes 6152 | tf_op jit(solution)/shard_map/ppermute | solution.py:14
  490.4 8.8 %collective-permute-start.26 = (f32[512]{0:T(512)S(1)}, f32[512]{0:T(512)S(1)}, u32[]{:S(2)}, u32[]{:S(2)}) collective-permute-start(f32[512]{0:T(512)S(1)} %multiply_add_fusion.14), channel_id=1, source_target_pairs={{8,0},{16,8},{24,16},{32,24},{40,32},{48,40},{56,48},{64,56},{72,6... | collective-permute-start | bytes 6152 | tf_op jit(solution)/shard_map/ppermute | solution.py:14
  499.2 8.8 %collective-permute-start.27 = (f32[512]{0:T(512)S(1)}, f32[512]{0:T(512)S(1)}, u32[]{:S(2)}, u32[]{:S(2)}) collective-permute-start(f32[512]{0:T(512)S(1)} %multiply_add_fusion.13), channel_id=1, source_target_pairs={{8,0},{16,8},{24,16},{32,24},{40,32},{48,40},{56,48},{64,56},{72,6... | collective-permute-start | bytes 6152 | tf_op jit(solution)/shard_map/ppermute | solution.py:14
  508.0 8.8 %collective-permute-start.28 = (f32[512]{0:T(512)S(1)}, f32[512]{0:T(512)S(1)}, u32[]{:S(2)}, u32[]{:S(2)}) collective-permute-start(f32[512]{0:T(512)S(1)} %multiply_add_fusion.12), channel_id=1, source_target_pairs={{8,0},{16,8},{24,16},{32,24},{40,32},{48,40},{56,48},{64,56},{72,6... | collective-permute-start | bytes 6152 | tf_op jit(solution)/shard_map/ppermute | solution.py:14
  516.8 8.8 %collective-permute-start.29 = (f32[512]{0:T(512)S(1)}, f32[512]{0:T(512)S(1)}, u32[]{:S(2)}, u32[]{:S(2)}) collective-permute-start(f32[512]{0:T(512)S(1)} %multiply_add_fusion.11), channel_id=1, source_target_pairs={{8,0},{16,8},{24,16},{32,24},{40,32},{48,40},{56,48},{64,56},{72,6... | collective-permute-start | bytes 6152 | tf_op jit(solution)/shard_map/ppermute | solution.py:14
  525.6 23.2 %collective-permute-start.30 = (f32[512]{0:T(512)S(1)}, f32[512]{0:T(512)S(1)}, u32[]{:S(2)}, u32[]{:S(2)}) collective-permute-start(f32[512]{0:T(512)S(1)} %multiply_add_fusion.10), channel_id=1, source_target_pairs={{8,0},{16,8},{24,16},{32,24},{40,32},{48,40},{56,48},{64,56},{72,6... | collective-permute-start | bytes 6152 | tf_op jit(solution)/shard_map/ppermute | solution.py:14
  534.9 16.3 %copy-start.1 = (bf16[512,512]{1,0:T(8,128)(2,1)S(1)}, bf16[512,512]{1,0:T(8,128)(2,1)}, u32[]{:S(2)}) copy-start(bf16[512,512]{1,0:T(8,128)(2,1)} %param.7) | copy-start | bytes 1572868
Sparse Core Ops, SparseCore 0:
  161.9 69.3 all-reduce.37
